TPU v7x, 32 devices: a whole 2x2x4 slice. The times are simulated.
32 devices in a mesh: dp: 4 (over x, core), tensor: 8 (over z, y).
Axes of the slice: x: 2, y: 2, z: 4, core: 2. Of those that a mesh axis runs over, the one named last changes fastest.
Arguments:
- hidden_in: bfloat16 [8192, 2048], P('dp'), may hold values from -6 to 6
- seq_lengths: int32 [4], P('dp'), may hold values from 1024 to 2048, as said below
- out_grad: bfloat16 [8192, 2048], P('dp'), may hold values from -6 to 6
- attn_gain: float32 [2048], replicated, may hold values from 0.5 to 1.5
- mlp_gain: float32 [2048], replicated, may hold values from 0.5 to 1.5
- w_query: bfloat16 [2048, 2048], P(None, 'tensor'), may hold values from -0.5 to 0.5
- w_key: bfloat16 [2048, 512], P('tensor'), may hold values from -0.5 to 0.5
- w_value: bfloat16 [2048, 512], P('tensor'), may hold values from -0.125 to 0.125
- w_out: bfloat16 [2048, 2048], P('tensor'), may hold values from -2 to 2
- w_gate: bfloat16 [2048, 8192], P(None, 'tensor'), may hold values from -0.125 to 0.125
- w_up: bfloat16 [2048, 8192], P(None, 'tensor'), may hold values from -0.125 to 0.125
- w_down: bfloat16 [8192, 2048], P('tensor'), may hold values from -0.5 to 0.5
Outputs:
- layer_out: bfloat16 [8192, 2048], P(('dp', 'tensor'))
- in_grad: float32 [8192, 2048], P(('dp', 'tensor'))
- attn_gain_grad: float32 [2048], P(('dp', 'tensor'))
- mlp_gain_grad: float32 [2048], P(('dp', 'tensor'))
- w_query_grad: float32 [2048, 2048], P('dp', 'tensor')
- w_key_grad: float32 [2048, 512], P(('dp', 'tensor'))
- w_value_grad: float32 [2048, 512], P(('dp', 'tensor'))
- w_out_grad: float32 [2048, 2048], P('tensor', 'dp')
- w_gate_grad: float32 [2048, 8192], P('dp', 'tensor')
- w_up_grad: float32 [2048, 8192], P('dp', 'tensor')
- w_down_grad: float32 [8192, 2048], P('tensor', 'dp')
Inputs may be any that keep to these rules, and one draw needn't show every extreme that they name: `seq_lengths`: each sequence has between half of its 2048 slots and all of them valid; some sequence is full and some is exactly half full.
All inputs are finite; a program needn't handle non-finite values.
Results may differ from a plain program's by a relative error of at most 0.02.
Values may be sent and summed in bfloat16 or wider, within the bound.
No kernel may reach another device: no remote copies, remote signals or barrier semaphores. Data moves between devices by JAX's collectives and lax.ppermute only.
A program may use at most 256 MiB of HBM per device.

v0:
```python
import math
import jax
import jax.numpy as jnp
from jax import lax
from jax.sharding import PartitionSpec as P

H = 32
KVH = 8
HD = 64
SEQ_LEN = 2048
QB = 512
RESID = 0.22
ATTN_SCALE = 0.015625
EPSILON = 1e-05
THETA_LOG = math.log(10000000.0)
MASKED = -1e30


def rope_tables(count):
    positions = (jnp.arange(count, dtype=jnp.int32) % SEQ_LEN).astype(jnp.float32)[:, None]
    freqs = jnp.exp(-THETA_LOG * jnp.arange(0, HD, 2, dtype=jnp.int32).astype(jnp.float32) / HD)[
        None, :
    ]
    angle_rows = positions * freqs
    angle_rows = jnp.concatenate([angle_rows, angle_rows], 1)
    return (jnp.cos(angle_rows), jnp.sin(angle_rows))


def turn_half(values):
    half = HD // 2
    return jnp.concatenate([-values[..., half:], values[..., :half]], -1)


def rotate(values, cosines, sines):
    return values * cosines[:, None, :] + turn_half(values) * sines[:, None, :]


def unrotate(grads, cosines, sines):
    return grads * cosines[:, None, :] - turn_half(grads * sines[:, None, :])


def norm_rows(rows, gain):
    row_scale = lax.rsqrt(jnp.mean(rows * rows, axis=-1, keepdims=True) + EPSILON)
    return (rows * row_scale * gain, row_scale)


def norm_back(rows, row_scale, gain, incoming):
    normed = rows * row_scale
    scaled = incoming * gain
    return row_scale * (scaled - normed * jnp.mean(scaled * normed, axis=-1, keepdims=True))


def local(
    hidden_in,
    seq_lengths,
    out_grad,
    attn_gain,
    mlp_gain,
    w_query,
    w_key,
    w_value,
    w_out,
    w_gate,
    w_up,
    w_down,
):
    rows_total = hidden_in.shape[0]
    heads_here = w_query.shape[1] // HD
    groups = lax.axis_size("tensor")
    member = lax.axis_index("tensor")
    share = rows_total // groups
    share_start = member * share
    blocks = rows_total // QB
    bf16 = jnp.bfloat16
    f32 = jnp.float32
    over_rows = (((0,), (0,)), ((), ()))
    over_cols = (((1,), (1,)), ((), ()))
    cosines, sines = rope_tables(rows_total)
    inputs = hidden_in.astype(f32)
    normed_one, scale_one = norm_rows(inputs, attn_gain)
    normed_low = normed_one.astype(bf16)
    key_all, value_all = (
        lax.all_gather(w_key, "tensor", axis=0, tiled=True),
        lax.all_gather(w_value, "tensor", axis=0, tiled=True),
    )
    kv_head = member * heads_here // (H // KVH)
    key_cols = lax.dynamic_slice_in_dim(key_all, kv_head * HD, HD, 1)
    value_cols = lax.dynamic_slice_in_dim(value_all, kv_head * HD, HD, 1)
    query_raw = jnp.dot(normed_low, w_query, preferred_element_type=f32).reshape(
        rows_total, heads_here, HD
    )
    key_raw = jnp.dot(normed_low, key_cols, preferred_element_type=f32)
    value_raw = jnp.dot(normed_low, value_cols, preferred_element_type=f32)
    queries = rotate(query_raw, cosines, sines).astype(bf16)
    keys = rotate(key_raw[:, None, :], cosines, sines)[:, 0, :].astype(bf16)
    values = value_raw.astype(bf16)
    seq_slots = jnp.arange(seq_lengths.shape[0], dtype=jnp.int32)

    def block_inputs(index):
        start = index * QB
        seq_index = start // SEQ_LEN
        key_start = seq_index * SEQ_LEN
        length = jnp.sum(jnp.where(seq_slots == seq_index, seq_lengths, 0))
        query_rows = lax.dynamic_slice_in_dim(queries, start, QB, 0)
        raw = jnp.einsum("qhd,kd->hqk", query_rows, keys, preferred_element_type=f32) * ATTN_SCALE
        query_pos = start - key_start + jnp.arange(QB, dtype=jnp.int32)
        key_pos = jnp.arange(SEQ_LEN, dtype=jnp.int32)
        allowed = (key_pos[None, :] <= query_pos[:, None]) & (key_pos[None, :] < length)
        scores = jnp.where(allowed[None], raw, MASKED)
        return (start, key_start, query_rows, keys, values, scores)

    def forward_block(index):
        start, key_start, query_rows, key_rows, value_rows, scores = block_inputs(index)
        highest = jnp.max(scores, axis=-1, keepdims=True)
        expos = jnp.exp(scores - highest)
        totals = jnp.sum(expos, axis=-1, keepdims=True)
        probs = (expos / totals).astype(bf16)
        block_out = jnp.einsum("hqk,kd->qhd", probs, value_rows, preferred_element_type=f32)
        return (block_out, (highest + jnp.log(totals))[..., 0])

    attn_blocks, lse_blocks = lax.map(forward_block, jnp.arange(blocks, dtype=jnp.int32))
    attended = attn_blocks.reshape(rows_total, heads_here * HD).astype(bf16)
    attn_part = jnp.dot(attended, w_out, preferred_element_type=f32)
    attn_share = lax.psum_scatter(attn_part, "tensor", scatter_dimension=0, tiled=True)
    inputs_share = lax.dynamic_slice_in_dim(inputs, share_start, share, 0)
    scale_one_share = lax.dynamic_slice_in_dim(scale_one, share_start, share, 0)
    attn_full = lax.all_gather(attn_share, "tensor", axis=0, tiled=True)
    middle = inputs + RESID * attn_full
    normed_two, scale_two = norm_rows(middle, mlp_gain)
    normed_two_low = normed_two.astype(bf16)
    middle_share = lax.dynamic_slice_in_dim(middle, share_start, share, 0)
    scale_two_share = lax.dynamic_slice_in_dim(scale_two, share_start, share, 0)
    gate_rows = jnp.dot(normed_two_low, w_gate, preferred_element_type=f32)
    up_rows = jnp.dot(normed_two_low, w_up, preferred_element_type=f32)
    sigmoid_gate = jax.nn.sigmoid(gate_rows)
    silu_gate = gate_rows * sigmoid_gate
    activ = (silu_gate * up_rows).astype(bf16)
    mlp_part = jnp.dot(activ, w_down, preferred_element_type=f32)
    mlp_share = lax.psum_scatter(
        mlp_part.astype(jnp.bfloat16), "tensor", scatter_dimension=0, tiled=True
    ).astype(jnp.float32)
    layer_out = (middle_share + RESID * mlp_share).astype(bf16)
    row_ids = jnp.arange(rows_total, dtype=jnp.int32)
    length_rows = jnp.sum(
        jnp.where((row_ids // SEQ_LEN)[:, None] == seq_slots[None, :], seq_lengths[None, :], 0),
        axis=1,
    )
    valid_rows = (row_ids % SEQ_LEN < length_rows).astype(f32)[:, None]
    cotangent = out_grad.astype(f32) * valid_rows
    down_in = (RESID * cotangent).astype(bf16)
    down_wgrad = lax.dot_general(activ, down_in, over_rows, preferred_element_type=f32)
    activ_grad = lax.dot_general(down_in, w_down, over_cols, preferred_element_type=f32)
    gate_grad = (
        activ_grad * up_rows * sigmoid_gate * (1.0 + gate_rows * (1.0 - sigmoid_gate))
    ).astype(bf16)
    up_grad = (activ_grad * silu_gate).astype(bf16)
    gate_wgrad = lax.dot_general(normed_two_low, gate_grad, over_rows, preferred_element_type=f32)
    up_wgrad = lax.dot_general(normed_two_low, up_grad, over_rows, preferred_element_type=f32)
    norm_two_part = lax.dot_general(gate_grad, w_gate, over_cols, preferred_element_type=f32)
    norm_two_part = norm_two_part + lax.dot_general(
        up_grad, w_up, over_cols, preferred_element_type=f32
    )
    norm_two_share = lax.psum_scatter(norm_two_part, "tensor", scatter_dimension=0, tiled=True)
    norm_two_full = lax.all_gather(norm_two_share, "tensor", axis=0, tiled=True)
    middle_grad = cotangent + norm_back(middle, scale_two, mlp_gain, norm_two_full)
    branch_grad = (RESID * middle_grad).astype(bf16)
    middle_grad_share = lax.dynamic_slice_in_dim(middle_grad, share_start, share, 0)
    mlp_gain_part = jnp.sum(norm_two_share * middle_share * scale_two_share, axis=0)
    out_wgrad = lax.dot_general(attended, branch_grad, over_rows, preferred_element_type=f32)
    attended_grad = lax.dot_general(branch_grad, w_out, over_cols, preferred_element_type=f32)
    attended_grad = attended_grad.reshape(rows_total, heads_here, HD).astype(bf16)

    def backward_block(carry, index):
        key_grad, value_grad = carry
        start, key_start, query_rows, key_rows, value_rows, scores = block_inputs(index)
        lse_rows = lax.dynamic_index_in_dim(lse_blocks, index, 0, keepdims=False)
        probs = jnp.exp(scores - lse_rows[:, :, None])
        probs_low = probs.astype(bf16)
        grad_rows = lax.dynamic_slice_in_dim(attended_grad, start, QB, 0)
        value_part = jnp.einsum("hqk,qhd->khd", probs_low, grad_rows, preferred_element_type=f32)
        prob_grad = jnp.einsum("qhd,kd->hqk", grad_rows, value_rows, preferred_element_type=f32)
        row_delta = jnp.sum(prob_grad * probs, axis=-1, keepdims=True)
        score_grad = (probs * (prob_grad - row_delta)).astype(bf16)
        query_part = (
            jnp.einsum("hqk,kd->qhd", score_grad, key_rows, preferred_element_type=f32) * ATTN_SCALE
        )
        key_part = (
            jnp.einsum("hqk,qhd->khd", score_grad, query_rows, preferred_element_type=f32)
            * ATTN_SCALE
        )
        key_grad = key_grad + key_part
        value_grad = value_grad + value_part
        return ((key_grad, value_grad), query_part)

    empty_grad = jnp.zeros((rows_total, heads_here, HD), f32)
    (key_grad, value_grad), query_blocks = lax.scan(
        backward_block, (empty_grad, empty_grad), jnp.arange(blocks, dtype=jnp.int32)
    )
    query_grad = query_blocks.reshape(rows_total, heads_here, HD)
    query_low = (
        unrotate(query_grad, cosines, sines).reshape(rows_total, heads_here * HD).astype(bf16)
    )
    key_low = unrotate(key_grad, cosines, sines).reshape(rows_total, heads_here * HD).astype(bf16)
    value_low = value_grad.reshape(rows_total, heads_here * HD).astype(bf16)
    width = normed_low.shape[1]
    query_wgrad = lax.dot_general(normed_low, query_low, over_rows, preferred_element_type=f32)
    key_head_grad = (
        lax.dot_general(normed_low, key_low, over_rows, preferred_element_type=f32)
        .reshape(width, heads_here, HD)
        .sum(axis=1)
    )
    value_head_grad = (
        lax.dot_general(normed_low, value_low, over_rows, preferred_element_type=f32)
        .reshape(width, heads_here, HD)
        .sum(axis=1)
    )
    key_tiled = jnp.tile(key_cols, (1, heads_here))
    value_tiled = jnp.tile(value_cols, (1, heads_here))
    norm_one_part = lax.dot_general(query_low, w_query, over_cols, preferred_element_type=f32)
    norm_one_part = norm_one_part + lax.dot_general(
        key_low, key_tiled, over_cols, preferred_element_type=f32
    )
    norm_one_part = norm_one_part + lax.dot_general(
        value_low, value_tiled, over_cols, preferred_element_type=f32
    )
    norm_one_share = lax.psum_scatter(
        norm_one_part.astype(jnp.bfloat16), "tensor", scatter_dimension=0, tiled=True
    ).astype(jnp.float32)
    in_grad = middle_grad_share + norm_back(
        inputs_share, scale_one_share, attn_gain, norm_one_share
    )
    attn_gain_part = jnp.sum(norm_one_share * inputs_share * scale_one_share, axis=0)
    key_full = lax.dynamic_update_slice_in_dim(
        jnp.zeros(key_all.shape, f32), key_head_grad, kv_head * HD, 1
    )
    value_full = lax.dynamic_update_slice_in_dim(
        jnp.zeros(value_all.shape, f32), value_head_grad, kv_head * HD, 1
    )
    dense = (
        lax.psum_scatter(
            query_wgrad.astype(jnp.bfloat16), "dp", scatter_dimension=0, tiled=True
        ).astype(jnp.float32),
        lax.psum_scatter(
            gate_wgrad.astype(jnp.bfloat16), "dp", scatter_dimension=0, tiled=True
        ).astype(jnp.float32),
        lax.psum_scatter(
            up_wgrad.astype(jnp.bfloat16), "dp", scatter_dimension=0, tiled=True
        ).astype(jnp.float32),
        lax.psum_scatter(
            out_wgrad.astype(jnp.bfloat16), "dp", scatter_dimension=1, tiled=True
        ).astype(jnp.float32),
        lax.psum_scatter(
            down_wgrad.astype(jnp.bfloat16), "dp", scatter_dimension=1, tiled=True
        ).astype(jnp.float32),
    )
    shared = (
        lax.psum_scatter(key_full, ("dp", "tensor"), scatter_dimension=0, tiled=True),
        lax.psum_scatter(value_full, ("dp", "tensor"), scatter_dimension=0, tiled=True),
        lax.psum_scatter(attn_gain_part, ("dp", "tensor"), scatter_dimension=0, tiled=True),
        lax.psum_scatter(mlp_gain_part, ("dp", "tensor"), scatter_dimension=0, tiled=True),
    )
    return (
        layer_out,
        in_grad,
        shared[2],
        shared[3],
        dense[0],
        shared[0],
        shared[1],
        dense[3],
        dense[1],
        dense[2],
        dense[4],
    )


def solution(mesh):
    placed = (
        P("dp", None),
        P("dp"),
        P("dp", None),
        P(),
        P(),
        P(None, "tensor"),
        P("tensor", None),
        P("tensor", None),
        P("tensor", None),
        P(None, "tensor"),
        P(None, "tensor"),
        P("tensor", None),
    )
    return jax.shard_map(
        local,
        mesh=mesh,
        in_specs=placed,
        out_specs=(
            P(("dp", "tensor"), None),
            P(("dp", "tensor"), None),
            P(("dp", "tensor")),
            P(("dp", "tensor")),
            P("dp", "tensor"),
            P(("dp", "tensor"), None),
            P(("dp", "tensor"), None),
            P("tensor", "dp"),
            P("dp", "tensor"),
            P("dp", "tensor"),
            P("tensor", "dp"),
        ),
        check_vma=False,
    )
```

profile of v0, /device:TPU:0, one launch (start us, length us, event | category | flops | bytes accessed | tf_op | source)
XLA Modules:
  0.0 2185.7 jit_solution(15121321370525812363)
XLA Ops:
  30.8 31.4 %all-gather.7.cloned.1.call-done = bf16[2048,512]{1,0:T(8,128)(2,1)} async-done(((bf16[256,512]{1,0:T(8,128)(2,1)}), bf16[2048,512]{1,0:T(8,128)(2,1)}) %all-gather.7.cloned.1.call-update) | async-done | bytes 2097168 | tf_op jit(solution)/shard_map/all_gather | solution.py:84
  62.2 49.9 %all-gather.5.cloned.1.call-done = bf16[2048,512]{1,0:T(8,128)(2,1)} async-done(((bf16[256,512]{1,0:T(8,128)(2,1)}), bf16[2048,512]{1,0:T(8,128)(2,1)}) %all-gather.5.cloned.1.call-update) | async-done | bytes 2097168 | tf_op jit(solution)/shard_map/all_gather | solution.py:83
  130.9 70.8 %while.31 = (s32[]{:T(128)}, bf16[4,512,4,64]{1,3,2,0:T(8,128)(2,1)}, f32[4,4,512]{2,1,0:T(4,128)}, s32[4]{0:T(128)S(1)}, s32[1]{0:T(128)}, /*index=5*/bf16[2048...) while((s32[]{:T(128)}, ...), condition=%wide.region_4.5_spmd, body=%wide.region_1.4_spmd.sunk | while | flops 1126171136 | bytes 64299484 | solution.py:121
  213.4 281.4 %reduce-scatter.12.cloned.1.call-done = f32[256,2048]{1,0:T(8,128)} async-done(((f32[2048,2048]{1,0:T(8,128)}), f32[256,2048]{1,0:T(8,128)}) %reduce-scatter.12.cloned.1.call-update) | async-done | bytes 2097168 | tf_op jit(solution)/shard_map/reduce_scatter | solution.py:124
  495.6 228.1 %all-gather.9.cloned.1.call-done = f32[2048,2048]{1,0:T(8,128)} async-done(((f32[256,2048]{1,0:T(8,128)}), f32[2048,2048]{1,0:T(8,128)}) %all-gather.9.cloned.1.call-update) | async-done | bytes 16777232 | tf_op jit(solution)/shard_map/all_gather | solution.py:127
  763.9 23.4 %multiply_convert_fusion.4 = (bf16[2048,1024]{1,0:T(8,128)(2,1)}, bf16[2048,1024]{1,0:T(8,128)(2,1)}, bf16[2048,1024]{1,0:T(8,128)(2,1)}) fusion(f32[2048,1024]{1,0:T(8,128)} %fusion.102, f32[2048,1024]{1,0:T(8,128)} %fusion.103, bf16[1024,2048]{1,0:T(8,128)(2,1)} %param.27, bf16[2048,2048]{1,0:T(8,128)(2,1)} %param.18, f32[2048]{0:T(1024)S(1)} %fusion.94), kind=kOutput, calls=%fused_computation.75 | convolution fusion | flops 8638169088 | bytes 41951232 | tf_op jit(solution)/shard_map/dot_general | solution.py:152
  787.3 15.3 fusion.104
  802.6 17.2 convolution_add_fusion
  819.9 281.0 %reduce-scatter.16.cloned.1.call-done = f32[256,2048]{1,0:T(8,128)} async-done(((f32[2048,2048]{1,0:T(8,128)}), f32[256,2048]{1,0:T(8,128)}) %reduce-scatter.16.cloned.1.call-update) | async-done | bytes 2097168 | tf_op jit(solution)/shard_map/reduce_scatter | solution.py:163
  1100.9 14.1 convolution_convert_fusion.3
  1115.1 14.2 convolution_convert_fusion.2
  1129.4 14.7 convolution_convert_fusion.1
  1146.1 14.4 convolution_convert_fusion
  1160.6 169.0 %all-gather.11.cloned.1.call-done = f32[2048,2048]{1,0:T(8,128)} async-done(((f32[256,2048]{1,0:T(8,128)}), f32[2048,2048]{1,0:T(8,128)}) %all-gather.11.cloned.1.call-update) | async-done | bytes 16777232 | tf_op jit(solution)/shard_map/all_gather | solution.py:164
  1329.5 13.7 multiply_reduce_fusion
  1343.2 15.7 multiply_add_fusion
  1365.0 302.1 %while.32 = (s32[]{:T(128)}, f32[2048,4,64]{0,2,1:T(8,128)}, f32[2048,4,64]{0,2,1:T(8,128)}, f32[4,512,4,64]{1,0,3,2:T(4,128)}, s32[4]{0:T(128)S(1)}, /*index=5*...) while((s32[]{:T(128)}, f32[2048,4,64]{0,2,1:T(8,128)}, ...), condition=%wide.region_12.13_spmd.clone, body=%wide.region_10.12_spmd.clone.sunk | while | flops 2752119296 | bytes 239403760 | solution.py:196
  1380.7 16.7 fusion.171
  1430.4 11.2 dynamic_update_slice.36
  1457.3 15.2 fusion.171
  1474.4 11.3 fusion.172
  1505.8 11.2 dynamic_update_slice.36
  1532.5 15.3 fusion.171
  1581.1 11.1 dynamic_update_slice.36
  1607.7 15.2 fusion.171
  1655.8 11.1 dynamic_update_slice.36
  1711.5 16.1 fusion.46
  1759.5 11.3 convert_element_type.153
  1788.2 99.2 %reduce-scatter.18.cloned.1.call-done = bf16[256,2048]{1,0:T(8,128)(2,1)} async-done(((bf16[2048,2048]{1,0:T(8,128)(2,1)}), bf16[256,2048]{1,0:T(8,128)(2,1)}) %reduce-scatter.18.cloned.1.call-update) | async-done | bytes 1048592 | tf_op jit(solution)/shard_map/reduce_scatter | solution.py:226
  1890.1 41.4 %all-reduce.2 = (f32[2048]{0:T(1024)S(1)}, f32[2048]{0:T(1024)S(1)}) all-reduce(f32[2048]{0:T(1024)S(1)} %get-tuple-element.295, f32[2048]{0:T(1024)S(1)} %get-tuple-element.343), channel_id=6, replica_groups=mesh['dp'=4,'tensor'=8] {'dp','tensor'}, use_global_device_ids=true, to_apply=%region_16.17.clone | all-reduce | flops 4096 | bytes 32768
  1937.1 96.4 %reduce-scatter.22.cloned.1.call-done = f32[64,512]{1,0:T(8,128)} async-done(((f32[2048,512]{1,0:T(8,128)}), f32[64,512]{1,0:T(8,128)}) %reduce-scatter.22.cloned.1.call-update) | async-done | bytes 131088 | tf_op jit(solution)/shard_map/reduce_scatter | solution.py:257
  2033.5 145.4 %reduce-scatter.24.cloned.1.call-done = f32[64,512]{1,0:T(8,128)} async-done(((f32[2048,512]{1,0:T(8,128)}), f32[64,512]{1,0:T(8,128)}) %reduce-scatter.24.cloned.1.call-update) | async-done | bytes 131088 | tf_op jit(solution)/shard_map/reduce_scatter | solution.py:258
  (360 shorter events, 439.1 us)
Async XLA Ops:
  7.2 198.0 %copy-start = (bf16[256,2048]{1,0:T(8,128)(2,1)S(1)}, bf16[256,2048]{1,0:T(8,128)(2,1)}, u32[]{:S(2)}) copy-start(bf16[256,2048]{1,0:T(8,128)(2,1)} %param.24) | copy-start | bytes 3145732
  7.2 55.0 %all-gather.7.cloned.1.call-start = ((), (), s32[]{:S(2)}) async-start(), calls=%async_computation.12 | async-start | bytes 2359296 | tf_op jit(solution)/shard_map/all_gather | solution.py:84
  7.9 104.2 %all-gather.5.cloned.1.call-start = ((), (), s32[]{:S(2)}) async-start(), calls=%async_computation.11 | async-start | bytes 2359296 | tf_op jit(solution)/shard_map/all_gather | solution.py:83
  8.7 486.1 %reduce-scatter.12.cloned.1.call-start = ((), (), s32[]{:S(2)}) async-start(), calls=%async_computation.13 | async-start | bytes 18874368 | tf_op jit(solution)/shard_map/reduce_scatter | solution.py:124
  213.3 510.3 %all-gather.9.cloned.1.call-start = ((), (), s32[]{:S(2)}) async-start(), calls=%async_computation.14 | async-start | bytes 18874368 | tf_op jit(solution)/shard_map/all_gather | solution.py:127
  494.8 606.0 %reduce-scatter.16.cloned.1.call-start = ((), (), s32[]{:S(2)}) async-start(), calls=%async_computation.16 | async-start | bytes 18874368 | tf_op jit(solution)/shard_map/reduce_scatter | solution.py:163
  495.5 244.1 %copy-start.33 = (f32[2048]{0:T(1024)S(1)}, f32[2048]{0:T(1024)}, u32[]{:S(2)}) copy-start(f32[2048]{0:T(1024)} %param.20) | copy-start | bytes 24580
  819.8 509.7 %all-gather.11.cloned.1.call-start = ((), (), s32[]{:S(2)}) async-start(), calls=%async_computation.17 | async-start | bytes 18874368 | tf_op jit(solution)/shard_map/all_gather | solution.py:164
  1100.9 671.7 %reduce-scatter.28.cloned.1.call-start = ((), (), s32[]{:S(2)}) async-start(), calls=%async_computation.23 | async-start | bytes 5242880 | tf_op jit(solution)/shard_map/reduce_scatter | solution.py:243
  1115.1 660.3 %reduce-scatter.30.cloned.1.call-start = ((), (), s32[]{:S(2)}) async-start(), calls=%async_computation.24 | async-start | bytes 5242880 | tf_op jit(solution)/shard_map/reduce_scatter | solution.py:246
  1129.4 648.9 %reduce-scatter.32.cloned.1.call-start = ((), (), s32[]{:S(2)}) async-start(), calls=%async_computation.25 | async-start | bytes 5242880 | tf_op jit(solution)/shard_map/reduce_scatter | solution.py:252
  1144.2 637.0 %reduce-scatter.14.cloned.1.call-start = ((), (), s32[]{:S(2)}) async-start(), calls=%async_computation.15 | async-start | bytes 9437184 | tf_op jit(solution)/shard_map/reduce_scatter | solution.py:139
  1160.5 169.0 %copy-start.30 = (f32[2048]{0:T(1024)S(1)}, f32[2048]{0:T(1024)}, u32[]{:S(2)}) copy-start(f32[2048]{0:T(1024)} %copy-done.29) | copy-start | bytes 24580
  1160.5 169.0 %copy-start.34 = (f32[2048]{0:T(1024)S(1)}, f32[2048]{0:T(1024)}, u32[]{:S(2)}) copy-start(f32[2048]{0:T(1024)} %param.20) | copy-start | bytes 24580
  1160.5 624.1 %reduce-scatter.20.cloned.1.call-start = ((), (), s32[]{:S(2)}) async-start(), calls=%async_computation.19 | async-start | bytes 1310720 | tf_op jit(solution)/shard_map/reduce_scatter | solution.py:240
  1380.7 16.7 slice-start
  1380.7 16.7 slice-start.1
  1380.7 18.1 slice-start.2
  1380.7 19.2 slice-start.3
  1457.3 15.9 slice-start.2
  1457.3 17.1 slice-start.3
  1485.7 15.8 slice-start.4
  1532.5 16.0 slice-start.2
  1532.5 17.2 slice-start.3
  1560.8 15.9 slice-start.4
  1607.7 15.9 slice-start.2
  1607.7 17.1 slice-start.3
  1683.9 102.5 %reduce-scatter.26.cloned.1.call-start = ((), (), s32[]{:S(2)}) async-start(), calls=%async_computation.22 | async-start | bytes 1310720 | tf_op jit(solution)/shard_map/reduce_scatter | solution.py:249
  1701.5 185.9 %reduce-scatter.18.cloned.1.call-start = ((), (), s32[]{:S(2)}) async-start(), calls=%async_computation.18 | async-start | bytes 9437184 | tf_op jit(solution)/shard_map/reduce_scatter | solution.py:226
  1727.6 306.0 %reduce-scatter.22.cloned.1.call-start = ((), (), s32[]{:S(2)}) async-start(), calls=%async_computation.20 | async-start | bytes 4325376 | tf_op jit(solution)/shard_map/reduce_scatter | solution.py:257
  1743.4 435.5 %reduce-scatter.24.cloned.1.call-start = ((), (), s32[]{:S(2)}) async-start(), calls=%async_computation.21 | async-start | bytes 4325376 | tf_op jit(solution)/shard_map/reduce_scatter | solution.py:258
  1772.5 114.8 %copy-start.32 = (f32[2048]{0:T(1024)S(1)}, f32[2048]{0:T(1024)}, u32[]{:S(2)}) copy-start(f32[2048]{0:T(1024)} %param.19) | copy-start | bytes 24580
  (69 other events, 532.6 us)
Sparse Core Ops, SparseCore 0:
  10.2 51.9 all-gather.6
  64.3 47.7 all-gather.4
  213.5 281.2 reduce-scatter.11
  497.0 226.6 all-gather.8
  819.9 280.8 reduce-scatter.15
  1102.8 226.6 all-gather.10
  1332.1 42.6 reduce-scatter.27
  1377.5 44.5 reduce-scatter.29
  1424.5 44.4 reduce-scatter.31
  1473.0 149.0 reduce-scatter.13
  1684.0 23.2 reduce-scatter.19
  1709.8 24.8 reduce-scatter.25
  1738.3 149.0 reduce-scatter.17
  1890.2 143.2 reduce-scatter.21
  2036.3 142.5 reduce-scatter.23
where the time goes:
time: 2200 us; the launch traced here: 2190 us
  waiting for transfers between devices  1380 us (63%)
  matrix products  437 us (20%)
  other arithmetic  178 us (8%)
  local copies, waits for them, and re-layouts  110 us (5%)
  blocking collectives  41.4 us (2%)
    reduce_scatter x1, waiting for transfers between devices, local(): lax.psum_scatter(attn_part, 'tensor', scatter_dimension=0, tiled=True)  281 us
    reduce_scatter x1, waiting for transfers between devices, local(): lax.psum_scatter(norm_two_part, 'tensor', scatter_dimension=0, tiled=True)  281 us
    all_gather x1, waiting for transfers between devices, local(): attn_full = lax.all_gather(attn_share, 'tensor', axis=0, tiled=True)  228 us
    all_gather x1, waiting for transfers between devices, local(): norm_two_full = lax.all_gather(norm_two_share, 'tensor', axis=0, tiled=True)  169 us
    reduce_scatter x1, waiting for transfers between devices, local(): lax.psum_scatter(value_full, ('dp', 'tensor'), scatter_dimension=0, tiled...  145 us
    reduce_scatter x1, waiting for transfers between devices, local(): lax.psum_scatter(norm_one_part.astype(jnp.bfloat16), 'tensor', scatter_di...  99.2 us
    reduce_scatter x1, waiting for transfers between devices, local(): lax.psum_scatter(key_full, ('dp', 'tensor'), scatter_dimension=0, tiled=T...  96.4 us
    dot_general x4, matrix products, backward_block(): jnp.einsum('qhd,kd->hqk', grad_rows, value_rows, preferred_element_type=f32)  62.5 us
  transfers between devices with their start and end apart: 15, of which 9 were waited for; matrix products, arithmetic and copies ran while one was open for 24% of the time, Pallas kernels for 0%

commit v1 on v0

--- a/solution.py
+++ b/solution.py
@@ -79,10 +79,28 @@
     inputs = hidden_in.astype(f32)
     normed_one, scale_one = norm_rows(inputs, attn_gain)
     normed_low = normed_one.astype(bf16)
-    key_all, value_all = (
-        lax.all_gather(w_key, "tensor", axis=0, tiled=True),
-        lax.all_gather(w_value, "tensor", axis=0, tiled=True),
-    )
+
+    def lay_lines(vec):
+        s_next, local_next, clean = (
+            lax.axis_size("tensor"),
+            lax.axis_index("tensor"),
+            vec.shape[0],
+        )
+        kept_arr, block_last = (vec, 1)
+        while block_last < s_next:
+            kept_arr = jnp.concatenate(
+                [
+                    kept_arr,
+                    lax.ppermute(
+                        kept_arr, "tensor", [(k, (k - block_last) % s_next) for k in range(s_next)]
+                    ),
+                ],
+                0,
+            )
+            block_last = 2 * block_last
+        return jnp.roll(kept_arr, local_next * clean, 0)
+
+    key_all, value_all = (lay_lines(w_key), lax.all_gather(w_value, "tensor", axis=0, tiled=True))
     kv_head = member * heads_here // (H // KVH)
     key_cols = lax.dynamic_slice_in_dim(key_all, kv_head * HD, HD, 1)
     value_cols = lax.dynamic_slice_in_dim(value_all, kv_head * HD, HD, 1)

time: 2200 us -> 2200 us (level)
    ppermute x0 -> x3, waiting for transfers between devices: none -> 71.4 us  [lay_lines(): lax.ppermute(kept_arr, 'tensor', [(k, (k - block_last) % s_next) for k in...]
    all_gather x1 -> x0, waiting for transfers between devices: 49.9 us -> none  [local(): lax.all_gather(w_key, 'tensor', axis=0, tiled=True)]
    all_gather x1, waiting for transfers between devices: 31.4 us -> 0.01 us  [local(): lax.all_gather(w_value, 'tensor', axis=0, tiled=True)]
  transfers between devices with their start and end apart: 15 -> 17, of which waited for: 9 -> 9; matrix products, arithmetic and copies ran while one was open for 24% -> 24% of each run, Pallas kernels for 0% -> 0%
where the time goes in v1:
time: 2200 us; the launch traced here: 2190 us
  waiting for transfers between devices  1380 us (63%)
  matrix products  435 us (20%)
  other arithmetic  179 us (8%)
  local copies, waits for them, and re-layouts  114 us (5%)
  blocking collectives  41.1 us (2%)
    reduce_scatter x1, waiting for transfers between devices, local(): lax.psum_scatter(attn_part, 'tensor', scatter_dimension=0, tiled=True)  283 us
    reduce_scatter x1, waiting for transfers between devices, local(): lax.psum_scatter(norm_two_part, 'tensor', scatter_dimension=0, tiled=True)  281 us
    all_gather x1, waiting for transfers between devices, local(): attn_full = lax.all_gather(attn_share, 'tensor', axis=0, tiled=True)  228 us
    all_gather x1, waiting for transfers between devices, local(): norm_two_full = lax.all_gather(norm_two_share, 'tensor', axis=0, tiled=True)  169 us
    reduce_scatter x1, waiting for transfers between devices, local(): lax.psum_scatter(value_full, ('dp', 'tensor'), scatter_dimension=0, tiled...  145 us
    reduce_scatter x1, waiting for transfers between devices, local(): lax.psum_scatter(norm_one_part.astype(jnp.bfloat16), 'tensor', scatter_di...  102 us
    reduce_scatter x1, waiting for transfers between devices, local(): lax.psum_scatter(key_full, ('dp', 'tensor'), scatter_dimension=0, tiled=T...  96.9 us
    ppermute x3, waiting for transfers between devices, lay_lines(): lax.ppermute(kept_arr, 'tensor', [(k, (k - block_last) % s_next) for k in...  71.4 us
  transfers between devices with their start and end apart: 17, of which 9 were waited for; matrix products, arithmetic and copies ran while one was open for 24% of the time, Pallas kernels for 0%

profile of v1, /device:TPU:0, one launch (start us, length us, event | category | flops | bytes accessed | tf_op | source)
XLA Modules:
  0.0 2188.0 jit_solution(13395437060146262256)
XLA Ops:
  51.1 60.6 %collective-permute-done.2 = bf16[1024,512]{1,0:T(8,128)(2,1)} collective-permute-done((bf16[1024,512]{1,0:T(8,128)(2,1)}, bf16[1024,512]{1,0:T(8,128)(2,1)}, u32[]{:S(2)}, u32[]{:S(2)}) %collective-permute-start.2) | collective-permute-done | bytes 1048608 | tf_op jit(solution)/shard_map/ppermute | solution.py:94
  134.7 69.5 %while.31 = (s32[]{:T(128)}, bf16[4,512,4,64]{1,3,2,0:T(8,128)(2,1)S(1)}, f32[4,4,512]{2,1,0:T(4,128)}, s32[4]{0:T(128)S(1)}, s32[1]{0:T(128)}, /*index=5*/bf16[...) while((s32[]{:T(128)}, ...), condition=%wide.region_4.5_spmd, body=%wide.region_1.4_spmd.sunk | while | flops 1126171136 | bytes 55910820 | solution.py:139
  214.6 282.5 %reduce-scatter.12.cloned.1.call-done = f32[256,2048]{1,0:T(8,128)} async-done(((f32[2048,2048]{1,0:T(8,128)}), f32[256,2048]{1,0:T(8,128)}) %reduce-scatter.12.cloned.1.call-update) | async-done | bytes 2097168 | tf_op jit(solution)/shard_map/reduce_scatter | solution.py:142
  497.8 228.3 %all-gather.6.cloned.1.call-done = f32[2048,2048]{1,0:T(8,128)} async-done(((f32[256,2048]{1,0:T(8,128)}), f32[2048,2048]{1,0:T(8,128)}) %all-gather.6.cloned.1.call-update) | async-done | bytes 16777232 | tf_op jit(solution)/shard_map/all_gather | solution.py:145
  766.1 23.4 %multiply_convert_fusion.4 = (bf16[2048,1024]{1,0:T(8,128)(2,1)}, bf16[2048,1024]{1,0:T(8,128)(2,1)}, bf16[2048,1024]{1,0:T(8,128)(2,1)}) fusion(f32[2048,1024]{1,0:T(8,128)} %fusion.101, f32[2048,1024]{1,0:T(8,128)} %fusion.102, bf16[1024,2048]{1,0:T(8,128)(2,1)} %param.27, bf16[2048,2048]{1,0:T(8,128)(2,1)} %param.18, f32[2048]{0:T(1024)S(1)} %fusion.93), kind=kOutput, calls=%fused_computation.75 | convolution fusion | flops 8638169088 | bytes 41951232 | tf_op jit(solution)/shard_map/dot_general | solution.py:170
  789.5 15.3 fusion.103
  804.8 17.2 convolution_add_fusion
  822.1 281.0 %reduce-scatter.16.cloned.1.call-done = f32[256,2048]{1,0:T(8,128)} async-done(((f32[2048,2048]{1,0:T(8,128)}), f32[256,2048]{1,0:T(8,128)}) %reduce-scatter.16.cloned.1.call-update) | async-done | bytes 2097168 | tf_op jit(solution)/shard_map/reduce_scatter | solution.py:181
  1103.2 14.1 convolution_convert_fusion.3
  1117.4 14.2 convolution_convert_fusion.2
  1131.7 14.7 convolution_convert_fusion.1
  1148.3 14.4 convolution_convert_fusion
  1162.8 168.9 %all-gather.8.cloned.1.call-done = f32[2048,2048]{1,0:T(8,128)} async-done(((f32[256,2048]{1,0:T(8,128)}), f32[2048,2048]{1,0:T(8,128)}) %all-gather.8.cloned.1.call-update) | async-done | bytes 16777232 | tf_op jit(solution)/shard_map/all_gather | solution.py:182
  1331.7 13.7 multiply_reduce_fusion
  1345.5 15.7 multiply_add_fusion
  1367.2 302.2 %while.32 = (s32[]{:T(128)}, f32[2048,4,64]{0,2,1:T(8,128)}, f32[2048,4,64]{0,2,1:T(8,128)}, f32[4,512,4,64]{1,0,3,2:T(4,128)}, s32[4]{0:T(128)S(1)}, /*index=5*...) while((s32[]{:T(128)}, f32[2048,4,64]{0,2,1:T(8,128)}, ...), condition=%wide.region_12.13_spmd.clone, body=%wide.region_10.12_spmd.clone.sunk | while | flops 2752119296 | bytes 239403760 | solution.py:214
  1382.9 16.7 fusion.171
  1432.7 11.2 dynamic_update_slice.36
  1459.5 15.2 fusion.171
  1476.5 11.3 fusion.172
  1508.0 11.2 dynamic_update_slice.36
  1534.7 15.4 fusion.171
  1551.9 11.1 fusion.172
  1583.3 11.1 dynamic_update_slice.36
  1609.9 15.2 fusion.171
  1658.0 11.1 dynamic_update_slice.36
  1711.8 16.1 fusion.46
  1759.2 11.3 convert_element_type.153
  1788.0 102.3 %reduce-scatter.18.cloned.1.call-done = bf16[256,2048]{1,0:T(8,128)(2,1)} async-done(((bf16[2048,2048]{1,0:T(8,128)(2,1)}), bf16[256,2048]{1,0:T(8,128)(2,1)}) %reduce-scatter.18.cloned.1.call-update) | async-done | bytes 1048592 | tf_op jit(solution)/shard_map/reduce_scatter | solution.py:244
  1893.0 41.1 %all-reduce.2 = (f32[2048]{0:T(1024)S(1)}, f32[2048]{0:T(1024)S(1)}) all-reduce(f32[2048]{0:T(1024)S(1)} %get-tuple-element.295, f32[2048]{0:T(1024)S(1)} %get-tuple-element.343), channel_id=6, replica_groups=mesh['dp'=4,'tensor'=8] {'dp','tensor'}, use_global_device_ids=true, to_apply=%region_16.17.clone | all-reduce | flops 4096 | bytes 32768
  1939.6 96.9 %reduce-scatter.22.cloned.1.call-done = f32[64,512]{1,0:T(8,128)} async-done(((f32[2048,512]{1,0:T(8,128)}), f32[64,512]{1,0:T(8,128)}) %reduce-scatter.22.cloned.1.call-update) | async-done | bytes 131088 | tf_op jit(solution)/shard_map/reduce_scatter | solution.py:275
  2036.5 144.7 %reduce-scatter.24.cloned.1.call-done = f32[64,512]{1,0:T(8,128)} async-done(((f32[2048,512]{1,0:T(8,128)}), f32[64,512]{1,0:T(8,128)}) %reduce-scatter.24.cloned.1.call-update) | async-done | bytes 131088 | tf_op jit(solution)/shard_map/reduce_scatter | solution.py:276
  (365 shorter events, 447.0 us)
Async XLA Ops:
  7.2 199.2 %copy-start = (bf16[256,2048]{1,0:T(8,128)(2,1)S(1)}, bf16[256,2048]{1,0:T(8,128)(2,1)}, u32[]{:S(2)}) copy-start(bf16[256,2048]{1,0:T(8,128)(2,1)} %param.24) | copy-start | bytes 3145732
  7.2 119.3 %all-gather.4.cloned.1.call-start = ((), (), s32[]{:S(2)}) async-start(), calls=%async_computation.11 | async-start | bytes 2359296 | tf_op jit(solution)/shard_map/all_gather | solution.py:103
  7.2 20.3 collective-permute-start
  13.3 483.8 %reduce-scatter.12.cloned.1.call-start = ((), (), s32[]{:S(2)}) async-start(), calls=%async_computation.12 | async-start | bytes 18874368 | tf_op jit(solution)/shard_map/reduce_scatter | solution.py:142
  28.3 16.8 collective-permute-start.1
  28.5 17.4 copy-start.22
  46.9 64.7 %collective-permute-start.2 = (bf16[1024,512]{1,0:T(8,128)(2,1)}, bf16[1024,512]{1,0:T(8,128)(2,1)}, u32[]{:S(2)}, u32[]{:S(2)}) collective-permute-start(bf16[1024,512]{1,0:T(8,128)(2,1)} %pad_maximum_fusion.1), channel_id=1, source_target_pairs={{0,4},{1,5},{2,6},{3,7},{4,0},{5,1},{6,2},{7,3},{8,12},{9,13},{10,... | collective-permute-start | bytes 3145736 | tf_op jit(solution)/shard_map/ppermute | solution.py:94
  48.7 64.2 %copy-start.23 = (bf16[256,512]{1,0:T(8,128)(2,1)S(1)}, bf16[256,512]{1,0:T(8,128)(2,1)}, u32[]{:S(2)}) copy-start(bf16[256,512]{1,0:T(8,128)(2,1)} %copy-done.21) | copy-start | bytes 786436
  48.7 64.3 %copy-start.16 = (bf16[512,512]{1,0:T(8,128)(2,1)S(1)}, bf16[512,512]{1,0:T(8,128)(2,1)}, u32[]{:S(2)}) copy-start(bf16[512,512]{1,0:T(8,128)(2,1)} %copy-done.15) | copy-start | bytes 1572868
  214.5 511.6 %all-gather.6.cloned.1.call-start = ((), (), s32[]{:S(2)}) async-start(), calls=%async_computation.13 | async-start | bytes 18874368 | tf_op jit(solution)/shard_map/all_gather | solution.py:145
  497.1 606.0 %reduce-scatter.16.cloned.1.call-start = ((), (), s32[]{:S(2)}) async-start(), calls=%async_computation.15 | async-start | bytes 18874368 | tf_op jit(solution)/shard_map/reduce_scatter | solution.py:181
  497.8 244.0 %copy-start.34 = (f32[2048]{0:T(1024)S(1)}, f32[2048]{0:T(1024)}, u32[]{:S(2)}) copy-start(f32[2048]{0:T(1024)} %param.20) | copy-start | bytes 24580
  822.0 509.7 %all-gather.8.cloned.1.call-start = ((), (), s32[]{:S(2)}) async-start(), calls=%async_computation.16 | async-start | bytes 18874368 | tf_op jit(solution)/shard_map/all_gather | solution.py:182
  1103.1 669.1 %reduce-scatter.28.cloned.1.call-start = ((), (), s32[]{:S(2)}) async-start(), calls=%async_computation.22 | async-start | bytes 5242880 | tf_op jit(solution)/shard_map/reduce_scatter | solution.py:261
  1117.3 657.7 %reduce-scatter.30.cloned.1.call-start = ((), (), s32[]{:S(2)}) async-start(), calls=%async_computation.23 | async-start | bytes 5242880 | tf_op jit(solution)/shard_map/reduce_scatter | solution.py:264
  1131.6 646.2 %reduce-scatter.32.cloned.1.call-start = ((), (), s32[]{:S(2)}) async-start(), calls=%async_computation.24 | async-start | bytes 5242880 | tf_op jit(solution)/shard_map/reduce_scatter | solution.py:270
  1146.4 634.4 %reduce-scatter.14.cloned.1.call-start = ((), (), s32[]{:S(2)}) async-start(), calls=%async_computation.14 | async-start | bytes 9437184 | tf_op jit(solution)/shard_map/reduce_scatter | solution.py:157
  1162.7 169.0 %copy-start.31 = (f32[2048]{0:T(1024)S(1)}, f32[2048]{0:T(1024)}, u32[]{:S(2)}) copy-start(f32[2048]{0:T(1024)} %copy-done.30) | copy-start | bytes 24580
  1162.7 169.0 %copy-start.35 = (f32[2048]{0:T(1024)S(1)}, f32[2048]{0:T(1024)}, u32[]{:S(2)}) copy-start(f32[2048]{0:T(1024)} %param.20) | copy-start | bytes 24580
  1162.7 621.6 %reduce-scatter.20.cloned.1.call-start = ((), (), s32[]{:S(2)}) async-start(), calls=%async_computation.18 | async-start | bytes 1310720 | tf_op jit(solution)/shard_map/reduce_scatter | solution.py:258
  1382.9 18.1 slice-start.2
  1382.9 19.3 slice-start.3
  1459.5 17.1 slice-start.3
  1534.7 17.2 slice-start.3
  1609.9 17.1 slice-start.3
  1686.5 99.6 %reduce-scatter.26.cloned.1.call-start = ((), (), s32[]{:S(2)}) async-start(), calls=%async_computation.21 | async-start | bytes 1310720 | tf_op jit(solution)/shard_map/reduce_scatter | solution.py:267
  1686.6 18.6 slice-start.6
  1686.6 18.6 slice-start.7
  1708.6 181.7 %reduce-scatter.18.cloned.1.call-start = ((), (), s32[]{:S(2)}) async-start(), calls=%async_computation.17 | async-start | bytes 9437184 | tf_op jit(solution)/shard_map/reduce_scatter | solution.py:244
  1728.0 308.6 %reduce-scatter.22.cloned.1.call-start = ((), (), s32[]{:S(2)}) async-start(), calls=%async_computation.19 | async-start | bytes 4325376 | tf_op jit(solution)/shard_map/reduce_scatter | solution.py:275
  1743.8 437.4 %reduce-scatter.24.cloned.1.call-start = ((), (), s32[]{:S(2)}) async-start(), calls=%async_computation.20 | async-start | bytes 4325376 | tf_op jit(solution)/shard_map/reduce_scatter | solution.py:276
  1772.2 118.1 %copy-start.33 = (f32[2048]{0:T(1024)S(1)}, f32[2048]{0:T(1024)}, u32[]{:S(2)}) copy-start(f32[2048]{0:T(1024)} %param.19) | copy-start | bytes 24580
  (67 other events, 587.8 us)
Sparse Core Ops, SparseCore 0:
  13.5 84.6 all-gather.3
  214.7 282.3 reduce-scatter.11
  499.4 226.6 all-gather.5
  822.1 280.9 reduce-scatter.15
  1105.1 226.6 all-gather.7
  1334.1 42.6 reduce-scatter.27
  1379.5 44.5 reduce-scatter.29
  1426.6 44.4 reduce-scatter.31
  1475.2 148.9 reduce-scatter.13
  1686.6 23.4 reduce-scatter.19
  1712.8 24.8 reduce-scatter.25
  1741.2 149.0 reduce-scatter.17
  1893.2 143.2 reduce-scatter.21
  2039.3 141.8 reduce-scatter.23
